TPU v7x, 32 devices: a whole 2x2x4 slice. The times are simulated.
32 devices in a mesh: sim: 8 (over y, x, core), ana: 4 (over z).
Axes of the slice: x: 2, y: 2, z: 4, core: 2. Of those that a mesh axis runs over, the one named last changes fastest.
Arguments:
- initial_disp: float32 [256, 512, 128], P('ana', 'sim'), may hold values from -24 to 24
- initial_vel: float32 [256, 512, 128], P('ana', 'sim'), may hold values from -2 to 2
- stiffness: float32 [512, 128], P('sim'), may hold values from 0.05 to 0.35
- basis: float32 [512, 128, 512], P(('sim', 'ana')), may hold values from -5 to 5
- rotation: float32 [768, 512], replicated, may hold values from -0.21875 to 0.21875
Outputs:
- basis_out: float32 [512, 128, 512], P(('sim', 'ana'))
- coords: float32 [512, 256], replicated
All inputs are finite; a program needn't handle non-finite values.
Results may differ from a plain program's by a relative error of at most 0.000054.
Values sent between devices are 32-bit elements; how exact they have to be, the bound alone decides.
No kernel may reach another device: no remote copies, remote signals or barrier semaphores. Data moves between devices by JAX's collectives and lax.ppermute only.
A program may use at most 64 MiB of HBM per device.

v0:
```python
import math
import jax
import jax.numpy as jnp
from jax import lax
from jax.sharding import PartitionSpec as P

M = 256
K = 512
STEPS = 4
epsilon = 1e-06


def with_halo(value, sides, width):
    for axis, dim in sides:
        size, length = (lax.axis_size(axis), value.shape[dim])
        up = [(i, (i + 1) % size) for i in range(size - 1)]
        down = [(j, i) for i, j in up]
        last = lax.slice_in_dim(value, length - width, length, axis=dim)
        initial = lax.slice_in_dim(value, 0, width, axis=dim)
        before = lax.ppermute(last, axis, up)
        after = lax.ppermute(initial, axis, down)
        value = jnp.concatenate([before, value, after], axis=dim)
    return value


def accelerate(displace, stiffness):
    padded = with_halo(displace, (("sim", 1),), 1)
    padded = jnp.pad(padded, ((0, 0), (0, 0), (1, 1)))
    laplace = (
        padded[:, 2:, 1:-1]
        + padded[:, :-2, 1:-1]
        + padded[:, 1:-1, 2:]
        + padded[:, 1:-1, :-2]
        - 4.0 * displace
    )
    return stiffness[None] * (
        laplace - 0.5 * displace * displace * displace / (1.0 + displace * displace)
    )


def contract(left, right, left_dim, right_dim):
    return lax.dot_general(
        left,
        right,
        (((left_dim,), (right_dim,)), ((), ())),
        precision=lax.Precision.HIGHEST,
        preferred_element_type=jnp.float32,
    )


def per_device(initial_disp, initial_vel, stiffness, basis, rotation):
    displace = initial_disp
    velocity = initial_vel
    for step_index in range(STEPS):
        velocity = velocity + accelerate(displace, stiffness)
        displace = displace + velocity
    row_count = basis.shape[0] * basis.shape[1] * lax.axis_size("sim") * lax.axis_size("ana")
    basis_rows = basis.reshape(-1, K)
    totals = lax.psum(jnp.sum(displace * displace, axis=(1, 2)), "sim")
    member_scale = jnp.sqrt(totals / row_count + epsilon)
    outgoing = displace / member_scale[:, None, None]
    arrived = lax.all_to_all(outgoing, "ana", split_axis=1, concat_axis=0, tiled=True)
    unscaled = arrived.reshape(M, -1)
    coefficients = lax.psum(contract(basis_rows, unscaled, 0, 1), ("sim", "ana")) / row_count
    remainder = unscaled - contract(coefficients, basis_rows, 0, 1)
    gram_matrix = lax.psum(contract(remainder, remainder, 1, 1), ("sim", "ana")) / row_count
    factor = jnp.linalg.cholesky(gram_matrix)
    fresh_basis = jax.scipy.linalg.solve_triangular(factor, remainder, lower=True)
    top_rows = rotation[:K]
    bottom_rows = rotation[K:]
    basis_out = contract(basis_rows, top_rows, 1, 0) + contract(fresh_basis, bottom_rows, 0, 0)
    coords = (
        contract(top_rows, coefficients, 0, 0) + contract(bottom_rows, factor, 0, 1)
    ) * math.sqrt(K)
    return (basis_out.reshape(basis.shape), coords)


def solution(mesh):
    in_specs = (
        P("ana", "sim", None),
        P("ana", "sim", None),
        P("sim", None),
        P(("sim", "ana"), None, None),
        P(),
    )
    out_specs = (P(("sim", "ana"), None, None), P())
    return jax.shard_map(
        per_device, mesh=mesh, in_specs=in_specs, out_specs=out_specs, check_vma=False
    )
```

profile of v0, /device:TPU:0, one launch (start us, length us, event | category | flops | bytes accessed | tf_op | source)
XLA Modules:
  0.0 476.9 jit_solution(9723111592130537525)
XLA Ops:
  7.2 2.8 copy.23
  10.0 1.3 collective-permute-start
  11.4 3.3 collective-permute-start.1
  16.7 5.5 %copy_add_fusion = (f32[64,64,128]{2,0,1:T(8,128)S(1)}, f32[64,64,128]{2,0,1:T(8,128)S(1)}) fusion(f32[64,64,128]{2,1,0:T(8,128)S(1)} %copy-done.3, f32[64,64,128]{2,0,1:T(8,128)S(1)} %copy.23, f32[64,66,130]{2,0,1:T(8,128)S(1)} %select_maximum_fusion.6, f32[64,1,128]{2,0,1:T(8,128)S(1)} %collective-permute-done.1, ...), kind=kLoop, calls=%fused_computation.118 | loop fusion | flops 8912896 | bytes 14778368 | tf_op jit(solution)/shard_map/add | solution.py:56
  22.2 1.3 collective-permute-start.2
  23.5 5.3 %collective-permute-start.3 = (f32[64,1,128]{2,0,1:T(8,128)S(1)}, f32[64,1,128]{2,0,1:T(8,128)S(1)}, u32[]{:S(2)}, u32[]{:S(2)}) collective-permute-start(f32[64,1,128]{2,0,1:T(8,128)S(1)} %get-tuple-element.36), channel_id=1, source_target_pairs={{0,4},{4,8},{8,12},{12,16},{16,20},{20,24},{24,28},{1,5},{5,9},{9,... | collective-permute-start | bytes 98312 | tf_op jit(solution)/shard_map/ppermute | solution.py:20
  30.8 1.9 fusion.67
  32.7 1.3 collective-permute-start.4
  34.0 5.0 %collective-permute-start.5 = (f32[64,1,128]{2,0,1:T(8,128)S(1)}, f32[64,1,128]{2,0,1:T(8,128)S(1)}, u32[]{:S(2)}, u32[]{:S(2)}) collective-permute-start(f32[64,1,128]{2,0,1:T(8,128)S(1)} %get-tuple-element.34), channel_id=1, source_target_pairs={{0,4},{4,8},{8,12},{12,16},{16,20},{20,24},{24,28},{1,5},{5,9},{9,... | collective-permute-start | bytes 98312 | tf_op jit(solution)/shard_map/ppermute | solution.py:20
  41.1 1.8 fusion.65
  42.9 1.3 collective-permute-start.6
  44.2 5.0 %collective-permute-start.7 = (f32[64,1,128]{2,0,1:T(8,128)S(1)}, f32[64,1,128]{2,0,1:T(8,128)S(1)}, u32[]{:S(2)}, u32[]{:S(2)}) collective-permute-start(f32[64,1,128]{2,0,1:T(8,128)S(1)} %get-tuple-element.32), channel_id=1, source_target_pairs={{0,4},{4,8},{8,12},{12,16},{16,20},{20,24},{24,28},{1,5},{5,9},{9,... | collective-permute-start | bytes 98312 | tf_op jit(solution)/shard_map/ppermute | solution.py:20
  51.3 2.0 multiply_reduce_fusion
  53.3 17.1 %psum.21 = f32[64]{0:T(128)S(1)} all-reduce(f32[64]{0:T(128)S(1)} %get-tuple-element.22), channel_id=1, replica_groups=mesh['sim'=8,'ana'=4] {'sim'}, use_global_device_ids=true, to_apply=%region_1.2 | all-reduce | flops 64 | bytes 512 | tf_op jit(solution)/shard_map/psum | solution.py:59
  70.7 53.3 %all_to_all.15 = f32[64,64,128]{2,0,1:T(8,128)S(1)} all-to-all(f32[64,64,128]{2,0,1:T(8,128)S(1)} %broadcast_divide_fusion), channel_id=1, replica_groups=mesh['sim'=8,'ana'=4] {'ana'}, dimensions={1} | all-to-all | bytes 4194304 | tf_op jit(solution)/shard_map/all_to_all | solution.py:62
  124.0 1.2 copy.24
  125.3 1.3 copy-done.2
  126.6 4.9 %fusion.34 = f32[512,256]{0,1:T(8,128)} fusion(f32[2048,512]{1,0:T(8,128)S(1)} %bitcast.54, f32[32,8,16,128]{3,2,1,0:T(8,128)S(1)} %bitcast.55), kind=kOutput, calls=%fused_computation.71 | convolution fusion | flops 3221225472 | bytes 6815744 | tf_op jit(solution)/shard_map/dot_general | solution.py:42
  131.5 128.3 %all-reduce.8.cloned.1.call-done = f32[512,256]{0,1:T(8,128)} async-done(((f32[512,256]{0,1:T(8,128)}), f32[512,256]{0,1:T(8,128)}) %all-reduce.8.cloned.1.call-update) | async-done | bytes 524304 | tf_op jit(solution)/shard_map/psum | solution.py:64
  259.9 7.1 %convolution_subtract_fusion = f32[256,2048]{1,0:T(8,128)S(1)} fusion(f32[2048,512]{1,0:T(8,128)} %bitcast.52, f32[32,8,16,128]{3,2,1,0:T(8,128)} %bitcast.56, f32[512,256]{0,1:T(8,128)} %all-reduce.8.cloned.1.call-done), kind=kOutput, calls=%fused_computation.18 | convolution fusion | flops 3221880832 | bytes 8912896 | tf_op jit(solution)/shard_map/dot_general | solution.py:42
  267.0 2.6 fusion.75
  269.6 10.3 %fusion.40 = f32[2048,512]{1,0:T(8,128)} fusion(f32[2048,512]{1,0:T(8,128)} %bitcast.53, f32[768,512]{1,0:T(8,128)} %param.9), kind=kOutput, calls=%fused_computation.77 | convolution fusion | flops 6442450944 | bytes 9437184 | tf_op jit(solution)/shard_map/dot_general | solution.py:42
  279.9 113.8 %all-reduce.10.cloned.1.call-done = f32[256,256]{0,1:T(8,128)} async-done(((f32[256,256]{0,1:T(8,128)}), f32[256,256]{0,1:T(8,128)}) %all-reduce.10.cloned.1.call-update) | async-done | bytes 262160 | tf_op jit(solution)/shard_map/psum | solution.py:66
  395.8 11.7 %cholesky.50 = f32[128,128]{1,0:T(8,128)S(1)} custom-call(f32[128,128]{1,0:T(8,128)S(1)} %cholesky.118), custom_call_target="Cholesky" | custom-call | tf_op jit(solution)/shard_map/jit(cholesky)/cholesky | solution.py:67
  407.6 9.8 %custom-call.15 = f32[1,128,128]{1,2,0:T(8,128)S(1)} custom-call(f32[1,128,128]{2,1,0:T(8,128)S(1)} %get-tuple-element.43), custom_call_target="InvertDiagBlocksLowerTriangular" | custom-call | tf_op jit(solution)/shard_map/jit(cholesky)/cholesky | solution.py:67
  417.9 11.7 %cholesky.105 = f32[128,128]{1,0:T(8,128)S(1)} custom-call(f32[128,128]{1,0:T(8,128)S(1)} %convolution_subtract_fusion.2), custom_call_target="Cholesky" | custom-call | tf_op jit(solution)/shard_map/jit(cholesky)/cholesky | solution.py:67
  431.7 1.8 fusion.42
  436.3 4.0 while.1
  437.2 1.3 bitcast_dynamic-update-slice_fusion.2
  439.1 1.3 bitcast_dynamic-update-slice_fusion.2
  440.4 19.7 %custom-call.16 = f32[2,128,128]{1,2,0:T(8,128)S(1)} custom-call(f32[2,128,128]{2,1,0:T(8,128)S(1)} %get-tuple-element.9), custom_call_target="InvertDiagBlocksLowerTriangular" | custom-call | tf_op jit(solution)/shard_map/jit(_solve_triangular)/triangular_solve | solution.py:68
  463.3 6.3 %convolution_add_fusion = f32[2048,512]{1,0:T(8,128)} fusion(f32[2048,512]{1,0:T(8,128)S(1)} %copy-done.1, f32[128,2048]{1,0:T(8,128)S(1)} %fusion.55, f32[128,2048]{1,0:T(8,128)S(1)} %fusion.37, f32[768,512]{1,0:T(8,128)} %param.9), kind=kOutput, calls=%fused_computation.13 | convolution fusion | flops 3222798336 | bytes 11010048 | tf_op jit(solution)/shard_map/dot_general | solution.py:42
  (62 shorter events, 19.2 us)
Async XLA Ops:
  7.2 252.7 %all-reduce.8.cloned.1.call-start = ((), (), s32[]{:S(2)}) async-start(), calls=%async_computation.1 | async-start | bytes 1048576 | tf_op jit(solution)/shard_map/psum | solution.py:64
  10.0 4.6 collective-permute-start
  11.3 5.4 %copy-start.3 = (f32[64,64,128]{2,1,0:T(8,128)S(1)}, f32[64,64,128]{2,1,0:T(8,128)}, u32[]{:S(2)}) copy-start(f32[64,64,128]{2,1,0:T(8,128)} %param.5) | copy-start | bytes 6291460
  11.3 5.4 %copy-start.5 = (f32[64,64,128]{2,1,0:T(8,128)S(1)}, f32[64,64,128]{2,1,0:T(8,128)}, u32[]{:S(2)}) copy-start(f32[64,64,128]{2,1,0:T(8,128)} %param.6) | copy-start | bytes 6291460
  11.4 5.4 %copy-start.8 = (f32[64,128]{1,0:T(8,128)S(1)}, f32[64,128]{1,0:T(8,128)}, u32[]{:S(2)}) copy-start(f32[64,128]{1,0:T(8,128)} %param.7) | copy-start | bytes 98308
  11.4 4.1 collective-permute-start.1
  22.2 6.6 %collective-permute-start.2 = (f32[64,1,128]{2,0,1:T(8,128)S(1)}, f32[64,1,128]{2,0,1:T(8,128)S(1)}, u32[]{:S(2)}, u32[]{:S(2)}) collective-permute-start(f32[64,1,128]{2,0,1:T(8,128)S(1)} %get-tuple-element.37), channel_id=1, source_target_pairs={{4,0},{8,4},{12,8},{16,12},{20,16},{24,20},{28,24},{5,1},{9,5},{13... | collective-permute-start | bytes 98312 | tf_op jit(solution)/shard_map/ppermute | solution.py:21
  23.5 6.1 %collective-permute-start.3 = (f32[64,1,128]{2,0,1:T(8,128)S(1)}, f32[64,1,128]{2,0,1:T(8,128)S(1)}, u32[]{:S(2)}, u32[]{:S(2)}) collective-permute-start(f32[64,1,128]{2,0,1:T(8,128)S(1)} %get-tuple-element.36), channel_id=1, source_target_pairs={{0,4},{4,8},{8,12},{12,16},{16,20},{20,24},{24,28},{1,5},{5,9},{9,... | collective-permute-start | bytes 98312 | tf_op jit(solution)/shard_map/ppermute | solution.py:20
  32.7 6.3 %collective-permute-start.4 = (f32[64,1,128]{2,0,1:T(8,128)S(1)}, f32[64,1,128]{2,0,1:T(8,128)S(1)}, u32[]{:S(2)}, u32[]{:S(2)}) collective-permute-start(f32[64,1,128]{2,0,1:T(8,128)S(1)} %get-tuple-element.35), channel_id=1, source_target_pairs={{4,0},{8,4},{12,8},{16,12},{20,16},{24,20},{28,24},{5,1},{9,5},{13... | collective-permute-start | bytes 98312 | tf_op jit(solution)/shard_map/ppermute | solution.py:21
  34.0 5.9 %collective-permute-start.5 = (f32[64,1,128]{2,0,1:T(8,128)S(1)}, f32[64,1,128]{2,0,1:T(8,128)S(1)}, u32[]{:S(2)}, u32[]{:S(2)}) collective-permute-start(f32[64,1,128]{2,0,1:T(8,128)S(1)} %get-tuple-element.34), channel_id=1, source_target_pairs={{0,4},{4,8},{8,12},{12,16},{16,20},{20,24},{24,28},{1,5},{5,9},{9,... | collective-permute-start | bytes 98312 | tf_op jit(solution)/shard_map/ppermute | solution.py:20
  42.9 6.3 %collective-permute-start.6 = (f32[64,1,128]{2,0,1:T(8,128)S(1)}, f32[64,1,128]{2,0,1:T(8,128)S(1)}, u32[]{:S(2)}, u32[]{:S(2)}) collective-permute-start(f32[64,1,128]{2,0,1:T(8,128)S(1)} %get-tuple-element.33), channel_id=1, source_target_pairs={{4,0},{8,4},{12,8},{16,12},{20,16},{24,20},{28,24},{5,1},{9,5},{13... | collective-permute-start | bytes 98312 | tf_op jit(solution)/shard_map/ppermute | solution.py:21
  44.2 5.9 %collective-permute-start.7 = (f32[64,1,128]{2,0,1:T(8,128)S(1)}, f32[64,1,128]{2,0,1:T(8,128)S(1)}, u32[]{:S(2)}, u32[]{:S(2)}) collective-permute-start(f32[64,1,128]{2,0,1:T(8,128)S(1)} %get-tuple-element.32), channel_id=1, source_target_pairs={{0,4},{4,8},{8,12},{12,16},{16,20},{20,24},{24,28},{1,5},{5,9},{9,... | collective-permute-start | bytes 98312 | tf_op jit(solution)/shard_map/ppermute | solution.py:20
  124.0 2.5 copy-start
  125.3 1.3 copy-start.2
  131.5 262.1 %all-reduce.10.cloned.1.call-start = ((), (), s32[]{:S(2)}) async-start(), calls=%async_computation.2 | async-start | bytes 524288 | tf_op jit(solution)/shard_map/psum | solution.py:66
  394.6 39.6 %copy-start.6 = (f32[512,256]{0,1:T(8,128)S(1)}, f32[512,256]{0,1:T(8,128)}, u32[]{:S(2)}) copy-start(f32[512,256]{0,1:T(8,128)} %all-reduce.8.cloned.1.call-done) | copy-start | bytes 1572868
  431.6 2.6 copy-start.4
  434.2 2.1 copy-start.7
  461.1 2.2 copy-start.1
Sparse Core Ops, SparseCore 0:
  131.6 128.2 all-reduce.7
  269.7 123.9 all-reduce.9
where the time goes:
time: 486 us; the launch traced here: 477 us
  waiting for transfers between devices  245 us (50%)
  other arithmetic  72.6 us (15%)
  blocking collectives  70.4 us (14%)
  matrix products  37.5 us (8%)
  starting transfers between devices  23.8 us (5%)
  between operations  16.2 us (3%)
  local copies, waits for them, and re-layouts  10.5 us (2%)
    psum x1, waiting for transfers between devices, per_device(): lax.psum(contract(basis_rows, unscaled, 0, 1), ('sim', 'ana')) / row_count  128 us
    psum x1, waiting for transfers between devices, per_device(): lax.psum(contract(remainder, remainder, 1, 1), ('sim', 'ana')) / row_count  114 us
    all_to_all x1, blocking collectives, per_device(): lax.all_to_all(outgoing, 'ana', split_axis=1, concat_axis=0, tiled=True)  53.3 us
    another operation x6, other arithmetic, per_device(): factor = jnp.linalg.cholesky(gram_matrix)  34 us
    dot_general x7, matrix products, contract(): lax.dot_general(left, right, (((left_dim,), (right_dim,)), ((), ())), pre...  33.9 us
    another operation x3, other arithmetic, per_device(): jax.scipy.linalg.solve_triangular(factor, remainder, lower=True)  20.4 us
    ppermute x4, starting transfers between devices, with_halo(): before = lax.ppermute(last, axis, up)  18.6 us
    psum x1, blocking collectives, per_device(): totals = lax.psum(jnp.sum(displace * displace, axis=(1, 2)), 'sim')  17.1 us
  transfers between devices with their start and end apart: 10, of which 6 were waited for; matrix products, arithmetic and copies ran while one was open for 2% of the time, Pallas kernels for 0%

commit v1 on v0

--- a/solution.py
+++ b/solution.py
@@ -8,6 +8,28 @@
 K = 512
 STEPS = 4
 epsilon = 1e-06
+
+
+def in_blocks(x, dim, length):
+    before, after = (x.shape[:dim], x.shape[dim + 1 :])
+    return jnp.moveaxis(x.reshape(*before, length, -1, *after), dim, 0)
+
+
+def laid_out(tiles, dim):
+    shape = list(tiles.shape[1:])
+    shape[dim] *= tiles.shape[0]
+    return jnp.moveaxis(tiles, 0, dim).reshape(shape)
+
+
+def pairwise_exchange(x, axis, split_dim, concat_dim):
+    size, mine = (lax.axis_size(axis), lax.axis_index(axis))
+    blocks = in_blocks(x, split_dim, size)
+    gathered = [blocks[mine]]
+    for step in range(1, size):
+        sent = blocks[mine ^ step]
+        gathered.append(lax.ppermute(sent, axis, [(i, i ^ step) for i in range(size)]))
+    blocks = jnp.stack(gathered)[mine ^ jnp.arange(size)]
+    return laid_out(blocks, concat_dim)
 
 
 def with_halo(value, sides, width):
@@ -59,7 +81,7 @@
     totals = lax.psum(jnp.sum(displace * displace, axis=(1, 2)), "sim")
     member_scale = jnp.sqrt(totals / row_count + epsilon)
     outgoing = displace / member_scale[:, None, None]
-    arrived = lax.all_to_all(outgoing, "ana", split_axis=1, concat_axis=0, tiled=True)
+    arrived = pairwise_exchange(outgoing, "ana", 1, 0)
     unscaled = arrived.reshape(M, -1)
     coefficients = lax.psum(contract(basis_rows, unscaled, 0, 1), ("sim", "ana")) / row_count
     remainder = unscaled - contract(coefficients, basis_rows, 0, 1)

time: 486 us -> 490 us (level)
  blocking collectives: 70.4 us -> 17.1 us
  waiting for transfers between devices: 245 us -> 291 us
  other arithmetic: 72.6 us -> 78.5 us
    all_to_all x1 -> x0, blocking collectives: 53.3 us -> none  [per_device(): lax.all_to_all(outgoing, 'ana', split_axis=1, concat_axis=0, tiled=True)]
    ppermute x0 -> x3, waiting for transfers between devices: none -> 35.4 us  [pairwise_exchange(): lax.ppermute(sent, axis, [(i, i ^ step) for i in range(size)])]
    psum x1, waiting for transfers between devices: 128 us -> 138 us  [per_device(): lax.psum(contract(basis_rows, unscaled, 0, 1), ('sim', 'ana')) / row_count]
  transfers between devices with their start and end apart: 10 -> 13, of which waited for: 6 -> 8; matrix products, arithmetic and copies ran while one was open for 2% -> 2% of each run, Pallas kernels for 0% -> 0%
where the time goes in v1:
time: 490 us; the launch traced here: 481 us
  waiting for transfers between devices  291 us (59%)
  other arithmetic  78.5 us (16%)
  matrix products  40.4 us (8%)
  starting transfers between devices  28.5 us (6%)
  blocking collectives  17.1 us (3%)
  between operations  16.3 us (3%)
  local copies, waits for them, and re-layouts  8.96 us (2%)
    psum x1, waiting for transfers between devices, per_device(): lax.psum(contract(basis_rows, unscaled, 0, 1), ('sim', 'ana')) / row_count  138 us
    psum x1, waiting for transfers between devices, per_device(): lax.psum(contract(remainder, remainder, 1, 1), ('sim', 'ana')) / row_count  114 us
    dot_general x7, matrix products, contract(): lax.dot_general(left, right, (((left_dim,), (right_dim,)), ((), ())), pre...  36.9 us
    ppermute x3, waiting for transfers between devices, pairwise_exchange(): lax.ppermute(sent, axis, [(i, i ^ step) for i in range(size)])  35.4 us
    another operation x6, other arithmetic, per_device(): factor = jnp.linalg.cholesky(gram_matrix)  34 us
    another operation x3, other arithmetic, per_device(): jax.scipy.linalg.solve_triangular(factor, remainder, lower=True)  20.4 us
    ppermute x4, starting transfers between devices, with_halo(): before = lax.ppermute(last, axis, up)  18.6 us
    psum x1, blocking collectives, per_device(): totals = lax.psum(jnp.sum(displace * displace, axis=(1, 2)), 'sim')  17.1 us
  transfers between devices with their start and end apart: 13, of which 8 were waited for; matrix products, arithmetic and copies ran while one was open for 2% of the time, Pallas kernels for 0%

profile of v1, /device:TPU:0, one launch (start us, length us, event | category | flops | bytes accessed | tf_op | source)
XLA Modules:
  0.0 481.0 jit_solution(5185057669884467563)
XLA Ops:
  9.6 3.3 collective-permute-start.1
  13.8 3.2 select_maximum_fusion.6
  17.0 2.2 fusion.70
  20.5 5.3 %collective-permute-start.3 = (f32[64,1,128]{2,1,0:T(1,128)S(1)}, f32[64,1,128]{2,1,0:T(1,128)S(1)}, u32[]{:S(2)}, u32[]{:S(2)}) collective-permute-start(f32[64,1,128]{2,1,0:T(1,128)S(1)} %get-tuple-element.38), channel_id=1, source_target_pairs={{0,4},{4,8},{8,12},{12,16},{16,20},{20,24},{24,28},{1,5},{5,9},{9,... | collective-permute-start | bytes 98312 | tf_op jit(solution)/shard_map/ppermute | solution.py:42
  26.7 1.6 select_maximum_fusion.4
  28.2 2.2 fusion.68
  31.8 5.0 %collective-permute-start.5 = (f32[64,1,128]{2,1,0:T(1,128)S(1)}, f32[64,1,128]{2,1,0:T(1,128)S(1)}, u32[]{:S(2)}, u32[]{:S(2)}) collective-permute-start(f32[64,1,128]{2,1,0:T(1,128)S(1)} %get-tuple-element.36), channel_id=1, source_target_pairs={{0,4},{4,8},{8,12},{12,16},{16,20},{20,24},{24,28},{1,5},{5,9},{9,... | collective-permute-start | bytes 98312 | tf_op jit(solution)/shard_map/ppermute | solution.py:42
  37.7 1.6 select_maximum_fusion.2
  39.3 3.2 fusion.66
  43.8 5.0 %collective-permute-start.7 = (f32[64,1,128]{2,1,0:T(1,128)S(1)}, f32[64,1,128]{2,1,0:T(1,128)S(1)}, u32[]{:S(2)}, u32[]{:S(2)}) collective-permute-start(f32[64,1,128]{2,1,0:T(1,128)S(1)} %get-tuple-element.34), channel_id=1, source_target_pairs={{0,4},{4,8},{8,12},{12,16},{16,20},{20,24},{24,28},{1,5},{5,9},{9,... | collective-permute-start | bytes 98312 | tf_op jit(solution)/shard_map/ppermute | solution.py:42
  49.6 1.6 select_maximum_fusion
  51.2 3.3 multiply_reduce_fusion
  54.5 17.1 %psum.21 = f32[64]{0:T(128)S(1)} all-reduce(f32[64]{0:T(128)S(1)} %get-tuple-element.20), channel_id=1, replica_groups=mesh['sim'=8,'ana'=4] {'sim'}, use_global_device_ids=true, to_apply=%region_1.2 | all-reduce | flops 64 | bytes 512 | tf_op jit(solution)/shard_map/psum | solution.py:81
  71.7 1.8 broadcast_divide_fusion
  73.8 1.6 collective-permute-start.8
  75.4 2.6 collective-permute-start.9
  78.2 20.4 %collective-permute-done.8 = f32[64,16,128]{2,1,0:T(8,128)S(1)} collective-permute-done((f32[64,16,128]{2,1,0:T(8,128)S(1)}, f32[64,16,128]{2,1,0:T(8,128)S(1)}, u32[]{:S(2)}, u32[]{:S(2)}) %collective-permute-start.8) | collective-permute-done | bytes 524320 | tf_op jit(solution)/shard_map/ppermute | solution.py:30
  98.6 15.0 %collective-permute-done.9 = f32[64,16,128]{2,1,0:T(8,128)S(1)} collective-permute-done((f32[64,16,128]{2,1,0:T(8,128)S(1)}, f32[64,16,128]{2,1,0:T(8,128)S(1)}, u32[]{:S(2)}, u32[]{:S(2)}) %collective-permute-start.9) | collective-permute-done | bytes 524320 | tf_op jit(solution)/shard_map/ppermute | solution.py:30
  115.1 2.3 gather_fusion
  117.4 7.8 %fusion.34 = f32[512,256]{0,1:T(8,128)} fusion(f32[2048,512]{1,0:T(8,128)} %bitcast.64, f32[32,8,16,128]{3,2,1,0:T(8,128)S(1)} %bitcast.67), kind=kOutput, calls=%fused_computation.73 | convolution fusion | flops 3221225472 | bytes 6815744 | tf_op jit(solution)/shard_map/dot_general | solution.py:64
  125.5 138.4 %all-reduce.8.cloned.1.call-done = f32[512,256]{0,1:T(8,128)} async-done(((f32[512,256]{0,1:T(8,128)}), f32[512,256]{0,1:T(8,128)}) %all-reduce.8.cloned.1.call-update) | async-done | bytes 524304 | tf_op jit(solution)/shard_map/psum | solution.py:86
  263.9 7.1 %convolution_subtract_fusion = f32[256,2048]{1,0:T(8,128)S(1)} fusion(f32[2048,512]{1,0:T(8,128)} %bitcast.65, f32[32,8,16,128]{3,2,1,0:T(8,128)} %bitcast.68, f32[512,256]{0,1:T(8,128)} %all-reduce.8.cloned.1.call-done), kind=kOutput, calls=%fused_computation.19 | convolution fusion | flops 3221880832 | bytes 8912896 | tf_op jit(solution)/shard_map/dot_general | solution.py:64
  271.0 2.6 fusion.77
  273.6 10.3 %fusion.40 = f32[2048,512]{1,0:T(8,128)} fusion(f32[2048,512]{1,0:T(8,128)} %bitcast.66, f32[768,512]{1,0:T(8,128)} %param.9), kind=kOutput, calls=%fused_computation.79 | convolution fusion | flops 6442450944 | bytes 9437184 | tf_op jit(solution)/shard_map/dot_general | solution.py:64
  283.9 113.7 %all-reduce.10.cloned.1.call-done = f32[256,256]{0,1:T(8,128)} async-done(((f32[256,256]{0,1:T(8,128)}), f32[256,256]{0,1:T(8,128)}) %all-reduce.10.cloned.1.call-update) | async-done | bytes 262160 | tf_op jit(solution)/shard_map/psum | solution.py:88
  399.8 11.7 %cholesky.50 = f32[128,128]{1,0:T(8,128)S(1)} custom-call(f32[128,128]{1,0:T(8,128)S(1)} %cholesky.118), custom_call_target="Cholesky" | custom-call | tf_op jit(solution)/shard_map/jit(cholesky)/cholesky | solution.py:89
  411.6 9.8 %custom-call.15 = f32[1,128,128]{1,2,0:T(8,128)S(1)} custom-call(f32[1,128,128]{2,1,0:T(8,128)S(1)} %get-tuple-element.45), custom_call_target="InvertDiagBlocksLowerTriangular" | custom-call | tf_op jit(solution)/shard_map/jit(cholesky)/cholesky | solution.py:89
  421.9 11.7 %cholesky.105 = f32[128,128]{1,0:T(8,128)S(1)} custom-call(f32[128,128]{1,0:T(8,128)S(1)} %convolution_subtract_fusion.2), custom_call_target="Cholesky" | custom-call | tf_op jit(solution)/shard_map/jit(cholesky)/cholesky | solution.py:89
  435.6 1.8 fusion.42
  440.3 4.2 while.1
  444.5 19.7 %custom-call.16 = f32[2,128,128]{1,2,0:T(8,128)S(1)} custom-call(f32[2,128,128]{2,1,0:T(8,128)S(1)} %get-tuple-element.9), custom_call_target="InvertDiagBlocksLowerTriangular" | custom-call | tf_op jit(solution)/shard_map/jit(_solve_triangular)/triangular_solve | solution.py:90
  467.4 6.2 %convolution_add_fusion = f32[2048,512]{1,0:T(8,128)} fusion(f32[2048,512]{1,0:T(8,128)S(1)} %copy-done, f32[128,2048]{1,0:T(8,128)S(1)} %fusion.55, f32[128,2048]{1,0:T(8,128)S(1)} %fusion.37, f32[768,512]{1,0:T(8,128)} %param.9), kind=kOutput, calls=%fused_computation.14 | convolution fusion | flops 3222798336 | bytes 11010048 | tf_op jit(solution)/shard_map/dot_general | solution.py:64
  (70 shorter events, 25.3 us)
Async XLA Ops:
  7.2 256.7 %all-reduce.8.cloned.1.call-start = ((), (), s32[]{:S(2)}) async-start(), calls=%async_computation | async-start | bytes 1048576 | tf_op jit(solution)/shard_map/psum | solution.py:86
  8.3 4.6 collective-permute-start
  9.6 7.4 %copy-start.2 = (f32[64,64,128]{2,1,0:T(8,128)S(1)}, f32[64,64,128]{2,1,0:T(8,128)}, u32[]{:S(2)}) copy-start(f32[64,64,128]{2,1,0:T(8,128)} %param.5) | copy-start | bytes 6291460
  9.6 7.4 %copy-start.6 = (f32[64,64,128]{2,1,0:T(8,128)S(1)}, f32[64,64,128]{2,1,0:T(8,128)}, u32[]{:S(2)}) copy-start(f32[64,64,128]{2,1,0:T(8,128)} %param.6) | copy-start | bytes 6291460
  9.6 7.3 %copy-start.8 = (f32[64,128]{1,0:T(8,128)S(1)}, f32[64,128]{1,0:T(8,128)}, u32[]{:S(2)}) copy-start(f32[64,128]{1,0:T(8,128)} %param.7) | copy-start | bytes 98308
  9.6 4.1 collective-permute-start.1
  19.2 6.6 %collective-permute-start.2 = (f32[64,1,128]{2,1,0:T(1,128)S(1)}, f32[64,1,128]{2,1,0:T(1,128)S(1)}, u32[]{:S(2)}, u32[]{:S(2)}) collective-permute-start(f32[64,1,128]{2,1,0:T(1,128)S(1)} %get-tuple-element.39), channel_id=1, source_target_pairs={{4,0},{8,4},{12,8},{16,12},{20,16},{24,20},{28,24},{5,1},{9,5},{13... | collective-permute-start | bytes 98312 | tf_op jit(solution)/shard_map/ppermute | solution.py:43
  20.5 6.1 %collective-permute-start.3 = (f32[64,1,128]{2,1,0:T(1,128)S(1)}, f32[64,1,128]{2,1,0:T(1,128)S(1)}, u32[]{:S(2)}, u32[]{:S(2)}) collective-permute-start(f32[64,1,128]{2,1,0:T(1,128)S(1)} %get-tuple-element.38), channel_id=1, source_target_pairs={{0,4},{4,8},{8,12},{12,16},{16,20},{20,24},{24,28},{1,5},{5,9},{9,... | collective-permute-start | bytes 98312 | tf_op jit(solution)/shard_map/ppermute | solution.py:42
  30.5 6.3 %collective-permute-start.4 = (f32[64,1,128]{2,1,0:T(1,128)S(1)}, f32[64,1,128]{2,1,0:T(1,128)S(1)}, u32[]{:S(2)}, u32[]{:S(2)}) collective-permute-start(f32[64,1,128]{2,1,0:T(1,128)S(1)} %get-tuple-element.37), channel_id=1, source_target_pairs={{4,0},{8,4},{12,8},{16,12},{20,16},{24,20},{28,24},{5,1},{9,5},{13... | collective-permute-start | bytes 98312 | tf_op jit(solution)/shard_map/ppermute | solution.py:43
  31.8 5.9 %collective-permute-start.5 = (f32[64,1,128]{2,1,0:T(1,128)S(1)}, f32[64,1,128]{2,1,0:T(1,128)S(1)}, u32[]{:S(2)}, u32[]{:S(2)}) collective-permute-start(f32[64,1,128]{2,1,0:T(1,128)S(1)} %get-tuple-element.36), channel_id=1, source_target_pairs={{0,4},{4,8},{8,12},{12,16},{16,20},{20,24},{24,28},{1,5},{5,9},{9,... | collective-permute-start | bytes 98312 | tf_op jit(solution)/shard_map/ppermute | solution.py:42
  42.5 6.4 %collective-permute-start.6 = (f32[64,1,128]{2,1,0:T(1,128)S(1)}, f32[64,1,128]{2,1,0:T(1,128)S(1)}, u32[]{:S(2)}, u32[]{:S(2)}) collective-permute-start(f32[64,1,128]{2,1,0:T(1,128)S(1)} %get-tuple-element.35), channel_id=1, source_target_pairs={{4,0},{8,4},{12,8},{16,12},{20,16},{24,20},{28,24},{5,1},{9,5},{13... | collective-permute-start | bytes 98312 | tf_op jit(solution)/shard_map/ppermute | solution.py:43
  43.8 5.9 %collective-permute-start.7 = (f32[64,1,128]{2,1,0:T(1,128)S(1)}, f32[64,1,128]{2,1,0:T(1,128)S(1)}, u32[]{:S(2)}, u32[]{:S(2)}) collective-permute-start(f32[64,1,128]{2,1,0:T(1,128)S(1)} %get-tuple-element.34), channel_id=1, source_target_pairs={{0,4},{4,8},{8,12},{12,16},{16,20},{20,24},{24,28},{1,5},{5,9},{9,... | collective-permute-start | bytes 98312 | tf_op jit(solution)/shard_map/ppermute | solution.py:42
  48.8 2.4 copy-start.3
  73.8 24.9 %collective-permute-start.8 = (f32[64,16,128]{2,1,0:T(8,128)S(1)}, f32[64,16,128]{2,1,0:T(8,128)S(1)}, u32[]{:S(2)}, u32[]{:S(2)}) collective-permute-start(f32[64,16,128]{2,1,0:T(8,128)S(1)} %get-tuple-element.33), channel_id=1, source_target_pairs={{0,1},{1,0},{2,3},{3,2},{4,5},{5,4},{6,7},{7,6},{8,9},{9,8},{10,11... | collective-permute-start | bytes 1572872 | tf_op jit(solution)/shard_map/ppermute | solution.py:30
  75.4 38.2 %collective-permute-start.9 = (f32[64,16,128]{2,1,0:T(8,128)S(1)}, f32[64,16,128]{2,1,0:T(8,128)S(1)}, u32[]{:S(2)}, u32[]{:S(2)}) collective-permute-start(f32[64,16,128]{2,1,0:T(8,128)S(1)} %get-tuple-element.32), channel_id=1, source_target_pairs={{0,2},{1,3},{2,0},{3,1},{4,6},{5,7},{6,4},{7,5},{8,10},{9,11},{10,... | collective-permute-start | bytes 1572872 | tf_op jit(solution)/shard_map/ppermute | solution.py:30
  78.0 35.6 %collective-permute-start.10 = (f32[64,16,128]{2,1,0:T(8,128)S(1)}, f32[64,16,128]{2,1,0:T(8,128)S(1)}, u32[]{:S(2)}, u32[]{:S(2)}) collective-permute-start(f32[64,16,128]{2,1,0:T(8,128)S(1)} %get-tuple-element.31), channel_id=1, source_target_pairs={{0,3},{1,2},{2,1},{3,0},{4,7},{5,6},{6,5},{7,4},{8,11},{9,10},{10,... | collective-permute-start | bytes 1572872 | tf_op jit(solution)/shard_map/ppermute | solution.py:30
  117.4 7.8 %copy-start.1 = (f32[4,64,16,128]{3,2,1,0:T(8,128)}, f32[4,64,16,128]{3,2,1,0:T(8,128)S(1)}, u32[]{:S(2)}) copy-start(f32[4,64,16,128]{3,2,1,0:T(8,128)S(1)} %gather_fusion) | copy-start | bytes 6291460
  125.2 272.4 %all-reduce.10.cloned.1.call-start = ((), (), s32[]{:S(2)}) async-start(), calls=%async_computation.1 | async-start | bytes 524288 | tf_op jit(solution)/shard_map/psum | solution.py:88
  398.6 39.5 %copy-start.5 = (f32[512,256]{0,1:T(8,128)S(1)}, f32[512,256]{0,1:T(8,128)}, u32[]{:S(2)}) copy-start(f32[512,256]{0,1:T(8,128)} %all-reduce.8.cloned.1.call-done) | copy-start | bytes 1572868
  435.6 2.6 copy-start.4
  438.2 2.1 copy-start.7
  465.2 2.2 copy-start
Sparse Core Ops, SparseCore 0:
  125.4 138.4 all-reduce.7
  273.7 123.9 all-reduce.9
